TPU v7x, 32 devices: a whole 2x2x4 slice. The times are simulated.
32 devices in a mesh: dp: 8 (over y, x, core), tensor: 4 (over z).
Axes of the slice: x: 2, y: 2, z: 4, core: 2. Of those that a mesh axis runs over, the one named last changes fastest.
Arguments:
- tokens: bfloat16 [8192, 2048], P('dp'), may hold values from -6 to 6
- cotangent: bfloat16 [8192, 2048], P('dp'), may hold values from -6 to 6
- segment_ids: int32 [8, 1024], P('dp'), may hold values from 0 to 2, never falling along the last dimension, each value on 1 to 768 neighbouring positions
- step_count: int32 [1], replicated, may hold values from 2 to 4
- norm_gains: float32 [2, 2048], P(None, 'dp'), may hold values from 0.5 to 1.5
- gains_first: float32 [2, 2048], P(None, 'dp'), may hold values from -0.0004272461 to 0.0004272461
- gains_second: float32 [2, 2048], P(None, 'dp'), may hold values from 9.5358565e-09 to 1.5211961e-07
- w_query: float32 [2048, 2048], P('dp', 'tensor'), may hold values from -0.125 to 0.125
- query_first: float32 [2048, 2048], P('dp', 'tensor'), may hold values from -0.00015258789 to 0.00015258789
- query_second: float32 [2048, 2048], P('dp', 'tensor'), may hold values from 1.4757873e-09 to 2.3839641e-08
- w_keyval: float32 [2, 2048, 256], P(None, 'dp', 'tensor'), may hold values from -0.125 to 0.125
- keyval_first: float32 [2, 2048, 256], P(None, 'dp', 'tensor'), may hold values from -0.0004272461 to 0.0004272461
- keyval_second: float32 [2, 2048, 256], P(None, 'dp', 'tensor'), may hold values from 1.0353215e-08 to 1.6710453e-07
- w_out: float32 [2048, 2048], P('tensor', 'dp'), may hold values from -1.5 to 1.5
- out_first: float32 [2048, 2048], P('tensor', 'dp'), may hold values from -1.5258789e-05 to 1.5258789e-05
- out_second: float32 [2048, 2048], P('tensor', 'dp'), may hold values from 1.7709447e-11 to 2.860757e-10
- w_gateup: float32 [2, 2048, 5632], P(None, 'dp', 'tensor'), may hold values from -0.125 to 0.125
- gateup_first: float32 [2, 2048, 5632], P(None, 'dp', 'tensor'), may hold values from -5.340576e-05 to 5.340576e-05
- gateup_second: float32 [2, 2048, 5632], P(None, 'dp', 'tensor'), may hold values from 1.4757873e-10 to 2.3839641e-09
- w_down: float32 [5632, 2048], P('tensor', 'dp'), may hold values from -0.15625 to 0.15625
- down_first: float32 [5632, 2048], P('tensor', 'dp'), may hold values from -4.5776367e-05 to 4.5776367e-05
- down_second: float32 [5632, 2048], P('tensor', 'dp'), may hold values from 1.1806298e-10 to 1.9071713e-09
Outputs:
- layer_out: bfloat16 [8192, 2048], P('dp')
- input_grad: float32 [8192, 2048], P('dp')
- grad_norm: float32 [1], replicated
- gains_moment: float32 [2, 2048], P(None, 'dp')
- gains_square: float32 [2, 2048], P(None, 'dp')
- gains_new: float32 [2, 2048], P(None, 'dp')
- query_moment: float32 [2048, 2048], P('dp', 'tensor')
- query_square: float32 [2048, 2048], P('dp', 'tensor')
- query_new: float32 [2048, 2048], P('dp', 'tensor')
- keyval_moment: float32 [2, 2048, 256], P(None, 'dp', 'tensor')
- keyval_square: float32 [2, 2048, 256], P(None, 'dp', 'tensor')
- keyval_new: float32 [2, 2048, 256], P(None, 'dp', 'tensor')
- out_moment: float32 [2048, 2048], P('tensor', 'dp')
- out_square: float32 [2048, 2048], P('tensor', 'dp')
- out_new: float32 [2048, 2048], P('tensor', 'dp')
- gateup_moment: float32 [2, 2048, 5632], P(None, 'dp', 'tensor')
- gateup_square: float32 [2, 2048, 5632], P(None, 'dp', 'tensor')
- gateup_new: float32 [2, 2048, 5632], P(None, 'dp', 'tensor')
- down_moment: float32 [5632, 2048], P('tensor', 'dp')
- down_square: float32 [5632, 2048], P('tensor', 'dp')
- down_new: float32 [5632, 2048], P('tensor', 'dp')
Inputs may be any that keep to these rules, and one draw needn't show every extreme that they name: `segment_ids`: in each batch row the segment ids never fall, all 3 ids occur, and the longest sequence of a row has 768 tokens; a token attends to the earlier tokens of its own sequence only.
All inputs are finite; a program needn't handle non-finite values.
Results may differ from a plain program's by a relative error of at most 0.017.
Values may be sent and summed in bfloat16 or wider, within the bound.
A program may use at most 320 MiB of HBM per device.

v0:
```python
import jax
import jax.numpy as jnp
from jax import lax
from jax.sharding import PartitionSpec as P

HD = 64
norm_eps = 1e-05
beta_first = 0.9
beta_second = 0.95
adam_eps = 1e-08
weight_decay = 0.1
weight_rate = 0.02
out_rate = 0.1
gain_rate = 0.2
clip_limit = 1.0
masked_value = -1000000000.0


def positions(segment):
    length = segment.shape[0]
    indices = jnp.arange(length, dtype=jnp.int32)
    earlier = jnp.concatenate([segment[:1] - 1, segment[:-1]])
    begins = jnp.where(segment != earlier, indices, jnp.zeros_like(indices))
    return indices - lax.cummax(begins, axis=0)


def rotary_tables(places, width):
    half_width = width // 2
    frequency = jnp.power(10000.0, -jnp.arange(half_width, dtype=jnp.float32) * (2.0 / width))
    angles = places.astype(jnp.float32)[:, None] * frequency[None, :]
    cosine_table = jnp.concatenate([jnp.cos(angles), jnp.cos(angles)], axis=-1)
    sine_table = jnp.concatenate([jnp.sin(angles), jnp.sin(angles)], axis=-1)
    return (cosine_table, sine_table)


def rotate(values, cosine_table, sine_table):
    half_width = values.shape[-1] // 2
    turned = jnp.concatenate([-values[..., half_width:], values[..., :half_width]], axis=-1)
    return values * cosine_table[:, None, :] + turned * sine_table[:, None, :]


def unrotate(gradient, cosine_table, sine_table):
    half_width = gradient.shape[-1] // 2
    along_sine = gradient * sine_table[:, None, :]
    turned = jnp.concatenate([along_sine[..., half_width:], -along_sine[..., :half_width]], axis=-1)
    return gradient * cosine_table[:, None, :] + turned


def over_rows(left, right):
    return lax.dot_general(
        left, right, (((0,), (0,)), ((), ())), preferred_element_type=jnp.float32
    )


def against(left, right):
    return lax.dot_general(
        left, right, (((1,), (1,)), ((), ())), preferred_element_type=jnp.float32
    )


def norm_back(grad_output, unit_rows, inverse, gain):
    scaled = grad_output * gain
    gain_grad = jnp.sum(grad_output * unit_rows, axis=0)
    inner_mean = jnp.mean(scaled * unit_rows, axis=-1, keepdims=True)
    return (inverse * (scaled - unit_rows * inner_mean), gain_grad)


def adam_step(weight, first, second, gradient, clip_factor, step_float, step_rate, decay_rate):
    gradient = gradient * clip_factor
    first = beta_first * first + (1.0 - beta_first) * gradient
    second = beta_second * second + (1.0 - beta_second) * gradient * gradient
    correct_one = 1.0 - jnp.power(beta_first, step_float)
    correct_two = 1.0 - jnp.power(beta_second, step_float)
    update = first / correct_one / (jnp.sqrt(second / correct_two) + adam_eps)
    return (first, second, weight - step_rate * (update + decay_rate * weight))


def on_device(
    tokens,
    cotangent,
    segment_ids,
    step_count,
    norm_gains,
    gains_first,
    gains_second,
    w_query,
    query_first,
    query_second,
    w_keyval,
    keyval_first,
    keyval_second,
    w_out,
    out_first,
    out_second,
    w_gateup,
    gateup_first,
    gateup_second,
    w_down,
    down_first,
    down_second,
):
    gathered = (
        lax.all_gather(norm_gains.astype(jnp.bfloat16), "dp", axis=1, tiled=True),
        lax.all_gather(w_query.astype(jnp.bfloat16), "dp", axis=0, tiled=True),
        lax.all_gather(w_keyval.astype(jnp.bfloat16), "dp", axis=1, tiled=True),
        lax.all_gather(w_out.astype(jnp.bfloat16), "dp", axis=1, tiled=True),
        lax.all_gather(w_gateup.astype(jnp.bfloat16), "dp", axis=1, tiled=True),
        lax.all_gather(w_down.astype(jnp.bfloat16), "dp", axis=1, tiled=True),
    )
    gain_rows, query_weight, keyval_weight, out_weight, gateup_weight, down_weight = gathered
    gain_values = gain_rows.astype(jnp.float32)
    length = tokens.shape[0]
    segment = segment_ids[0]
    local_heads = query_weight.shape[1] // HD
    local_groups = keyval_weight.shape[2] // HD
    group_size = local_heads // local_groups
    cosine_table, sine_table = rotary_tables(positions(segment), HD)
    indices = jnp.arange(length, dtype=jnp.int32)
    block_rows = min(512, length)
    starts = jnp.arange(length // block_rows, dtype=jnp.int32) * block_rows
    inverse_scale = HD ** (-0.5)
    values_in = tokens.astype(jnp.float32)
    inverse_one = lax.rsqrt(jnp.mean(values_in * values_in, axis=-1, keepdims=True) + norm_eps)
    unit_one = values_in * inverse_one
    normed_one = (unit_one * gain_values[0]).astype(jnp.bfloat16)
    query_raw = jnp.dot(normed_one, query_weight, preferred_element_type=jnp.float32)
    queries = rotate(query_raw.reshape(length, local_heads, HD), cosine_table, sine_table).astype(
        jnp.bfloat16
    )
    queries = queries.reshape(length, local_groups, group_size, HD)
    keyval_raw = jnp.einsum(
        "nd,sdk->snk", normed_one, keyval_weight, preferred_element_type=jnp.float32
    )
    key_rows = rotate(
        keyval_raw[0].reshape(length, local_groups, HD), cosine_table, sine_table
    ).astype(jnp.bfloat16)
    value_rows = keyval_raw[1].reshape(length, local_groups, HD).astype(jnp.bfloat16)

    def block_scores(start):
        query_block = lax.dynamic_slice_in_dim(queries, start, block_rows, 0)
        segment_block = lax.dynamic_slice_in_dim(segment, start, block_rows, 0)
        row_index = start + jnp.arange(block_rows, dtype=jnp.int32)
        allowed = (segment_block[:, None] == segment[None, :]) & (
            row_index[:, None] >= indices[None, :]
        )
        raw_scores = jnp.einsum(
            "qkgh,pkh->kgqp", query_block, key_rows, preferred_element_type=jnp.float32
        )
        return (query_block, jnp.where(allowed, raw_scores * inverse_scale, masked_value))

    def forward_block(start):
        query_block, scaled = block_scores(start)
        highest = jnp.max(scaled, axis=-1, keepdims=True)
        lifted = jnp.exp(scaled - highest)
        row_total = jnp.sum(lifted, axis=-1, keepdims=True)
        soft_weights = (lifted / row_total).astype(jnp.bfloat16)
        mixed = jnp.einsum(
            "kgqp,pkh->qkgh", soft_weights, value_rows, preferred_element_type=jnp.float32
        )
        return (
            mixed.astype(jnp.bfloat16).reshape(block_rows, local_heads * HD),
            (highest + jnp.log(row_total))[..., 0],
        )

    mixed_blocks, logsum_blocks = lax.map(forward_block, starts)
    mixture = mixed_blocks.reshape(length, local_heads * HD)
    branch_partial = jnp.dot(mixture, out_weight, preferred_element_type=jnp.float32)
    branch = lax.psum(branch_partial, "tensor")
    middle = values_in + branch
    inverse_two = lax.rsqrt(jnp.mean(middle * middle, axis=-1, keepdims=True) + norm_eps)
    unit_two = middle * inverse_two
    normed_two = (unit_two * gain_values[1]).astype(jnp.bfloat16)
    gateup = jnp.einsum(
        "nd,sdf->snf", normed_two, gateup_weight, preferred_element_type=jnp.float32
    )
    hidden = (jax.nn.silu(gateup[0]) * gateup[1]).astype(jnp.bfloat16)
    feed_out = lax.psum(
        jnp.dot(hidden, down_weight, preferred_element_type=jnp.float32).astype(jnp.bfloat16),
        "tensor",
    ).astype(jnp.float32)
    layer_out = (middle + feed_out).astype(jnp.bfloat16)
    regathered = (
        lax.all_gather(norm_gains.astype(jnp.bfloat16), "dp", axis=1, tiled=True),
        lax.all_gather(w_query.astype(jnp.bfloat16), "dp", axis=0, tiled=True),
        lax.all_gather(w_keyval.astype(jnp.bfloat16), "dp", axis=1, tiled=True),
        lax.all_gather(w_out.astype(jnp.bfloat16), "dp", axis=1, tiled=True),
        lax.all_gather(w_gateup.astype(jnp.bfloat16), "dp", axis=1, tiled=True),
        lax.all_gather(w_down.astype(jnp.bfloat16), "dp", axis=1, tiled=True),
    )
    gain_rows, query_weight, keyval_weight, out_weight, gateup_weight, down_weight = regathered
    gain_values = gain_rows.astype(jnp.float32)
    grad_down_weight = over_rows(hidden, cotangent)
    grad_hidden = against(cotangent, down_weight)
    gate_values = gateup[0]
    up_values = gateup[1]
    sigmoid_gate = jax.nn.sigmoid(gate_values)
    grad_gate = grad_hidden * up_values * sigmoid_gate * (1.0 + gate_values * (1.0 - sigmoid_gate))
    grad_up = grad_hidden * gate_values * sigmoid_gate
    grad_gateup = jnp.stack([grad_gate, grad_up]).astype(jnp.bfloat16)
    grad_gateup_weight = jnp.einsum(
        "nd,snf->sdf", normed_two, grad_gateup, preferred_element_type=jnp.float32
    )
    partial_two = jnp.einsum(
        "snf,sdf->nd", grad_gateup, gateup_weight, preferred_element_type=jnp.float32
    )
    grad_normed_two = lax.psum(partial_two, "tensor")
    grad_from_two, gain_grad_two = norm_back(grad_normed_two, unit_two, inverse_two, gain_values[1])
    grad_middle = cotangent.astype(jnp.float32) + grad_from_two
    grad_branch = grad_middle.astype(jnp.bfloat16)
    grad_out_weight = over_rows(mixture, grad_branch)
    grad_mixture = (
        against(grad_branch, out_weight)
        .astype(jnp.bfloat16)
        .reshape(length, local_groups, group_size, HD)
    )

    def backward_block(carried, pieces):
        start, logsum = pieces
        query_block, scaled = block_scores(start)
        soft_weights = jnp.exp(scaled - logsum[..., None])
        grad_block = lax.dynamic_slice_in_dim(grad_mixture, start, block_rows, 0)
        grad_soft = jnp.einsum(
            "qkgh,pkh->kgqp", grad_block, value_rows, preferred_element_type=jnp.float32
        )
        spread = jnp.sum(soft_weights * grad_soft, axis=-1, keepdims=True)
        grad_scores = (soft_weights * (grad_soft - spread) * inverse_scale).astype(jnp.bfloat16)
        grad_query = jnp.einsum(
            "kgqp,pkh->qkgh", grad_scores, key_rows, preferred_element_type=jnp.float32
        )
        grad_key = carried[0] + jnp.einsum(
            "kgqp,qkgh->pkh", grad_scores, query_block, preferred_element_type=jnp.float32
        )
        grad_value = carried[1] + jnp.einsum(
            "kgqp,qkgh->pkh",
            soft_weights.astype(jnp.bfloat16),
            grad_block,
            preferred_element_type=jnp.float32,
        )
        return ((grad_key, grad_value), grad_query)

    zero_rows = jnp.zeros((length, local_groups, HD), jnp.float32)
    (grad_keys, grad_values), grad_queries = lax.scan(
        backward_block, (zero_rows, zero_rows), (starts, logsum_blocks)
    )
    grad_queries = grad_queries.reshape(length, local_heads, HD)
    grad_query_raw = (
        unrotate(grad_queries, cosine_table, sine_table)
        .astype(jnp.bfloat16)
        .reshape(length, local_heads * HD)
    )
    grad_key_raw = unrotate(grad_keys, cosine_table, sine_table).reshape(length, local_groups * HD)
    grad_keyval = jnp.stack([grad_key_raw, grad_values.reshape(length, local_groups * HD)]).astype(
        jnp.bfloat16
    )
    grad_query_weight = over_rows(normed_one, grad_query_raw)
    grad_keyval_weight = jnp.einsum(
        "nd,snk->sdk", normed_one, grad_keyval, preferred_element_type=jnp.float32
    )
    partial_one = against(grad_query_raw, query_weight) + jnp.einsum(
        "snk,sdk->nd", grad_keyval, keyval_weight, preferred_element_type=jnp.float32
    )
    grad_normed_one = lax.psum(partial_one.astype(jnp.bfloat16), "tensor").astype(jnp.float32)
    grad_from_one, gain_grad_one = norm_back(grad_normed_one, unit_one, inverse_one, gain_values[0])
    input_grad = grad_middle + grad_from_one
    gain_grads = jnp.stack([gain_grad_one, gain_grad_two])
    reduced = (
        lax.psum_scatter(gain_grads, "dp", scatter_dimension=1, tiled=True),
        lax.psum_scatter(grad_query_weight, "dp", scatter_dimension=0, tiled=True),
        lax.psum_scatter(grad_keyval_weight, "dp", scatter_dimension=1, tiled=True),
        lax.psum_scatter(grad_out_weight, "dp", scatter_dimension=1, tiled=True),
        lax.psum_scatter(grad_gateup_weight, "dp", scatter_dimension=1, tiled=True),
        lax.psum_scatter(grad_down_weight, "dp", scatter_dimension=1, tiled=True),
    )
    first_owner = (lax.axis_index("tensor") == 0).astype(jnp.float32)
    local_square = first_owner * jnp.sum(reduced[0] * reduced[0]) + sum(
        (jnp.sum(g * g) for g in reduced[1:])
    )
    square_total = lax.psum(local_square, ("dp", "tensor"))
    grad_norm = jnp.sqrt(square_total)
    clip_factor = jnp.minimum(1.0, clip_limit / (grad_norm + 1e-06))
    step_float = step_count[0].astype(jnp.float32)
    params = (norm_gains, w_query, w_keyval, w_out, w_gateup, w_down)
    states = (
        (gains_first, gains_second),
        (query_first, query_second),
        (keyval_first, keyval_second),
        (out_first, out_second),
        (gateup_first, gateup_second),
        (down_first, down_second),
    )
    step_rates = (gain_rate, weight_rate, weight_rate, out_rate, weight_rate, weight_rate)
    decay_rates = (0.0, weight_decay, weight_decay, weight_decay, weight_decay, weight_decay)
    results = []
    for position_index in range(6):
        first, second = states[position_index]
        results.extend(
            adam_step(
                params[position_index],
                first,
                second,
                reduced[position_index],
                clip_factor,
                step_float,
                step_rates[position_index],
                decay_rates[position_index],
            )
        )
    return (
        layer_out,
        input_grad,
        grad_norm.reshape(1),
        results[0],
        results[1],
        results[2],
        results[3],
        results[4],
        results[5],
        results[6],
        results[7],
        results[8],
        results[9],
        results[10],
        results[11],
        results[12],
        results[13],
        results[14],
        results[15],
        results[16],
        results[17],
    )


def solution(mesh):
    in_specs = (
        P("dp", None),
        P("dp", None),
        P("dp", None),
        P(),
        P(None, "dp"),
        P(None, "dp"),
        P(None, "dp"),
        P("dp", "tensor"),
        P("dp", "tensor"),
        P("dp", "tensor"),
        P(None, "dp", "tensor"),
        P(None, "dp", "tensor"),
        P(None, "dp", "tensor"),
        P("tensor", "dp"),
        P("tensor", "dp"),
        P("tensor", "dp"),
        P(None, "dp", "tensor"),
        P(None, "dp", "tensor"),
        P(None, "dp", "tensor"),
        P("tensor", "dp"),
        P("tensor", "dp"),
        P("tensor", "dp"),
    )
    out_specs = (
        P("dp", None),
        P("dp", None),
        P(),
        P(None, "dp"),
        P(None, "dp"),
        P(None, "dp"),
        P("dp", "tensor"),
        P("dp", "tensor"),
        P("dp", "tensor"),
        P(None, "dp", "tensor"),
        P(None, "dp", "tensor"),
        P(None, "dp", "tensor"),
        P("tensor", "dp"),
        P("tensor", "dp"),
        P("tensor", "dp"),
        P(None, "dp", "tensor"),
        P(None, "dp", "tensor"),
        P(None, "dp", "tensor"),
        P("tensor", "dp"),
        P("tensor", "dp"),
        P("tensor", "dp"),
    )
    return jax.shard_map(
        on_device, mesh=mesh, in_specs=in_specs, out_specs=out_specs, check_vma=False
    )
```

profile of v0, /device:TPU:0, one launch (start us, length us, event | category | flops | bytes accessed | tf_op | source)
XLA Modules:
  0.0 1800.6 jit_solution(3728736641630619204)
XLA Ops:
  11.8 10.5 all_gather.24
  26.0 14.2 all_gather.26
  51.2 37.7 %while.28 = (s32[]{:T(128)}, bf16[2,512,512]{2,1,0:T(8,128)(2,1)}, f32[2,1,8,512]{3,2,1,0:T(8,128)}, s32[2]{0:T(128)S(1)}, s32[1024]{0:T(1024)S(1)}, /*index=5*/...) while((s32[]{:T(128)}, bf16[2,512,512]{2,1,0:T(8,128)(2,1)}, ...), condition=%wide.region_6.7_spmd.clone, body=%wide.region_3.6_spmd.clone.sunk | while | flops 1125904896 | bytes 64371432 | solution.py:165
  88.9 7.7 fusion.122
  100.9 287.2 %all-reduce.5.cloned.1.call-done = f32[1024,2048]{1,0:T(8,128)} async-done(((f32[1024,2048]{1,0:T(8,128)}), f32[1024,2048]{1,0:T(8,128)}) %all-reduce.5.cloned.1.call-update) | async-done | bytes 8388624 | tf_op jit(solution)/shard_map/psum | solution.py:168
  388.1 9.2 multiply_reduce_fusion.2
  397.4 59.8 %all-gather.9.cloned.1.call-done = bf16[2,2048,1408]{2,1,0:T(8,128)(2,1)} async-done(((bf16[2,256,1408]{2,1,0:T(8,128)(2,1)}), bf16[2,2048,1408]{2,1,0:T(8,128)(2,1)}) %all-gather.9.cloned.1.call-update) | async-done | bytes 11534352 | tf_op jit(solution)/shard_map/all_gather | solution.py:107
  457.2 20.2 %convolution_bitcast_fusion.3 = f32[2,1024,1408]{2,1,0:T(8,128)} fusion(bf16[2,2048,1408]{2,1,0:T(8,128)(2,1)} %all-gather.9.cloned.1.call-done, f32[1024,2048]{1,0:T(8,128)} %get-tuple-element.339, f32[2048]{0:T(1024)S(1)} %bitcast.364, f32[1024]{0:T(1024)S(1)} %add_rsqrt_fusion), kind=kOutput, calls=%fused_computation.85 | convolution fusion | flops 11817451520 | bytes 31469568 | tf_op jit(solution)/shard_map/nd,sdf->snf/dot_general | solution.py:173
  477.4 26.5 %all-gather.11.cloned.1.call-done = bf16[1408,2048]{1,0:T(8,128)(2,1)} async-done(((bf16[1408,256]{1,0:T(8,128)(2,1)}), bf16[1408,2048]{1,0:T(8,128)(2,1)}) %all-gather.11.cloned.1.call-update) | async-done | bytes 5767184 | tf_op jit(solution)/shard_map/all_gather | solution.py:108
  503.9 15.6 fusion.71
  522.0 17.0 convolution_bitcast_fusion.4
  539.1 11.3 convolution_convert_fusion
  550.4 279.6 %all-reduce.7.cloned.1.call-done = f32[1024,2048]{1,0:T(8,128)} async-done(((f32[1024,2048]{1,0:T(8,128)}), f32[1024,2048]{1,0:T(8,128)}) %all-reduce.7.cloned.1.call-update) | async-done | bytes 8388624 | tf_op jit(solution)/shard_map/psum | solution.py:206
  830.0 7.6 multiply_reduce_fusion
  850.9 129.5 %while.29 = (s32[]{:T(128)}, f32[1024,1,64]{0,2,1:T(8,128)}, f32[1024,1,64]{0,2,1:T(8,128)}, f32[2,512,1,8,64]{1,0,4,3,2:T(2,128)}, s32[2]{0:T(128)S(1)}, /*inde...) while((s32[]{:T(128)}, f32[1024,1,64]{0,2,1:T(8,128)}, ...), condition=%wide.region_14.15_spmd.clone, body=%wide.region_12.14_spmd.clone.sunk | while | flops 2728129024 | bytes 178878960 | solution.py:242
  859.7 10.8 fusion.181
  882.7 19.5 %dynamic_update_slice.22 = f32[2,512,1,8,64]{1,0,4,3,2:T(2,128)} dynamic-update-slice(f32[2,512,1,8,64]{1,0,4,3,2:T(2,128)} %get-tuple-element.553, f32[1,512,1,8,64]{1,0,4,3,2:T(1,128)S(1)} %copy.99, s32[]{:T(128)} %get-tuple-element.550, s32[]{:T(128)} %constant.54.clone.1..sunk.1, s32[]{:T(128)} %constant.54.clone.1..sunk.1, s32[]{:T(128)} %constant.54.clone.1..sunk.1, s32[]{:T(128)} %constant.54.clone.1..sunk.1) | dynamic-update-slice | bytes 2097156 | tf_op jit(solution)/shard_map/while/body/jit(dynamic_update_index_in_dim)/dynamic_update_slice | solution.py:242
  924.4 10.8 fusion.181
  947.4 19.5 %dynamic_update_slice.22 = f32[2,512,1,8,64]{1,0,4,3,2:T(2,128)} dynamic-update-slice(f32[2,512,1,8,64]{1,0,4,3,2:T(2,128)} %get-tuple-element.553, f32[1,512,1,8,64]{1,0,4,3,2:T(1,128)S(1)} %copy.99, s32[]{:T(128)} %get-tuple-element.550, s32[]{:T(128)} %constant.54.clone.1..sunk.1, s32[]{:T(128)} %constant.54.clone.1..sunk.1, s32[]{:T(128)} %constant.54.clone.1..sunk.1, s32[]{:T(128)} %constant.54.clone.1..sunk.1) | dynamic-update-slice | bytes 2097156 | tf_op jit(solution)/shard_map/while/body/jit(dynamic_update_index_in_dim)/dynamic_update_slice | solution.py:242
  972.1 7.6 fusion.184
  1008.6 7.8 fusion.78
  1016.5 269.4 %all-reduce.9.cloned.1.call-done = (bf16[1024,2048]{1,0:T(8,128)(2,1)}, bf16[1024,2048]{1,0:T(8,128)(2,1)}) async-done(((bf16[1024,2048]{1,0:T(8,128)(2,1)}, bf16[1024,2048]{1,0:T(8,128)(2,1)}), (bf16[1024,2048]{1,0:T(8,128)(2,1)}, bf16[1024,2048]{1,0:T(8,128)(2,1)})) %all-reduce.9.cloned.1.call-update) | async-done | bytes 8388624 | tf_op jit(solution)/shard_map/psum | solution.py:177
  1292.4 11.3 fusion.124
  1304.4 21.0 %convolution_bitcast_fusion.2 = f32[2,2048,1408]{1,2,0:T(8,128)} fusion(bf16[1,1024,1408]{2,1,0:T(8,128)(2,1)} %copy-done.62, bf16[1,1024,1408]{2,1,0:T(8,128)(2,1)} %copy-done.61, f32[1024,2048]{1,0:T(8,128)} %get-tuple-element.339, f32[2048]{0:T(1024)S(1)} %bitcast.367, f32[1024]{0:T(1024)S(1)} %copy-done.52), kind=kOutput, calls=%fused_computation.61 | convolution fusion | flops 11820335104 | bytes 37236736 | tf_op jit(solution)/shard_map/nd,snf->sdf/dot_general | solution.py:200
  1337.5 42.0 %reduce-scatter.9.cloned.1.call-done = f32[256,512]{1,0:T(8,128)} async-done(((f32[2048,512]{1,0:T(8,128)}), f32[256,512]{1,0:T(8,128)}) %reduce-scatter.9.cloned.1.call-update) | async-done | bytes 524304 | tf_op jit(solution)/shard_map/reduce_scatter | solution.py:268
  1382.5 51.9 %reduce-scatter.13.cloned.1.call-done = f32[512,256]{1,0:T(8,128)} async-done(((f32[512,2048]{1,0:T(8,128)}), f32[512,256]{1,0:T(8,128)}) %reduce-scatter.13.cloned.1.call-update) | async-done | bytes 524304 | tf_op jit(solution)/shard_map/reduce_scatter | solution.py:270
  1436.8 9.5 fusion.60
  1446.3 27.9 %reduce-scatter.19.cloned.1.call-done = f32[256,2]{1,0:T(8,128)} async-done(((f32[2048,2]{1,0:T(8,128)}), f32[256,2]{1,0:T(8,128)}) %reduce-scatter.19.cloned.1.call-update) | async-done | bytes 2064
  1476.4 87.9 %reduce-scatter.17.cloned.1.call-done = f32[1408,256]{1,0:T(8,128)} async-done(((f32[1408,2048]{1,0:T(8,128)}), f32[1408,256]{1,0:T(8,128)}) %reduce-scatter.17.cloned.1.call-update) | async-done | bytes 1441808 | tf_op jit(solution)/shard_map/reduce_scatter | solution.py:272
  1566.7 147.2 %reduce-scatter.15.cloned.1.call-done = f32[2,256,1408]{1,2,0:T(8,128)} async-done(((f32[2,2048,1408]{1,2,0:T(8,128)}), f32[2,256,1408]{1,2,0:T(8,128)}) %reduce-scatter.15.cloned.1.call-update) | async-done | bytes 2883600 | tf_op jit(solution)/shard_map/reduce_scatter | solution.py:271
  1718.4 8.4 add_convert_fusion
  1726.8 39.5 %psum.39 = f32[]{:T(128)} all-reduce(f32[]{:T(128)S(6)} %add.273), channel_id=1, replica_groups=mesh['dp'=8,'tensor'=4] {'dp','tensor'}, use_global_device_ids=true, to_apply=%region_31.32 | all-reduce | flops 1 | bytes 8 | tf_op jit(solution)/shard_map/psum | solution.py:278
  (292 shorter events, 211.2 us)
Async XLA Ops:
  7.2 18.8 %copy-start.37 = (f32[2,256,64]{1,2,0:T(8,128)S(1)}, f32[2,256,64]{1,2,0:T(8,128)}, u32[]{:S(2)}) copy-start(f32[2,256,64]{1,2,0:T(8,128)} %param.36) | copy-start | bytes 393220
  7.2 37.9 %all-gather.5.cloned.1.call-start = ((), (), s32[]{:S(2)}) async-start(), calls=%async_computation.6 | async-start | bytes 2359296 | tf_op jit(solution)/shard_map/all_gather | solution.py:104
  9.1 79.8 %all-gather.7.cloned.1.call-start = ((), (), s32[]{:S(2)}) async-start(), calls=%async_computation.7 | async-start | bytes 2359296 | tf_op jit(solution)/shard_map/all_gather | solution.py:106
  10.9 377.2 %all-reduce.5.cloned.1.call-start = ((), (), s32[]{:S(2)}) async-start(), calls=%async_computation.8 | async-start | bytes 16777216 | tf_op jit(solution)/shard_map/psum | solution.py:168
  11.0 29.3 %copy-start.2 = (bf16[1024,2048]{1,0:T(8,128)(2,1)S(1)}, bf16[1024,2048]{1,0:T(8,128)(2,1)}, u32[]{:S(2)}) copy-start(bf16[1024,2048]{1,0:T(8,128)(2,1)} %param.26) | copy-start | bytes 12582916
  22.9 22.1 %copy-start.47 = (f32[1,2048]{1,0:T(1,128)}, f32[1,2048]{1,0:T(1,128)S(1)}, u32[]{:S(2)}) copy-start(f32[1,2048]{1,0:T(1,128)S(1)} %get-tuple-element.356) | copy-start | bytes 24580
  26.0 19.0 %copy-start.53 = (f32[1024]{0:T(1024)}, f32[1024]{0:T(1024)S(1)}, u32[]{:S(2)}) copy-start(f32[1024]{0:T(1024)S(1)} %add_rsqrt_fusion.1) | copy-start | bytes 12292
  88.9 7.7 copy-start.17
  96.6 360.6 %all-gather.9.cloned.1.call-start = ((), (), s32[]{:S(2)}) async-start(), calls=%async_computation.9 | async-start | bytes 12976128 | tf_op jit(solution)/shard_map/all_gather | solution.py:107
  99.9 404.0 %all-gather.11.cloned.1.call-start = ((), (), s32[]{:S(2)}) async-start(), calls=%async_computation.10 | async-start | bytes 6488064 | tf_op jit(solution)/shard_map/all_gather | solution.py:108
  100.9 356.3 %copy-start.49 = (f32[1,2048]{1,0:T(1,128)S(1)}, f32[1,2048]{1,0:T(1,128)}, u32[]{:S(2)}) copy-start(f32[1,2048]{1,0:T(1,128)} %get-tuple-element.355) | copy-start | bytes 24580
  100.9 729.1 %all-reduce.7.cloned.1.call-start = ((), (), s32[]{:S(2)}) async-start(), calls=%async_computation.11 | async-start | bytes 16777216 | tf_op jit(solution)/shard_map/psum | solution.py:206
  397.4 440.3 %copy-start.51 = (f32[1024]{0:T(1024)}, f32[1024]{0:T(1024)S(1)}, u32[]{:S(2)}) copy-start(f32[1024]{0:T(1024)S(1)} %add_rsqrt_fusion) | copy-start | bytes 12292
  539.1 746.9 %all-reduce.9.cloned.1.call-start = ((), (), s32[]{:S(2)}) async-start(), calls=%async_computation.18 | async-start | bytes 16777216 | tf_op jit(solution)/shard_map/psum | solution.py:177
  830.0 8.2 copy-start.5
  830.0 9.4 copy-start.18
  839.5 8.1 copy-start.60
  881.6 20.6 %copy-start.7 = (f32[1024,1,64]{0,2,1:T(8,128)S(1)}, f32[1024,1,64]{0,2,1:T(8,128)}, u32[]{:S(2)}) copy-start(f32[1024,1,64]{0,2,1:T(8,128)} %get-tuple-element.551) | copy-start | bytes 786436 | tf_op jit(solution)/shard_map/while
  907.4 7.6 copy-start.8
  907.4 8.3 copy-start.4
  946.3 20.6 %copy-start.7 = (f32[1024,1,64]{0,2,1:T(8,128)S(1)}, f32[1024,1,64]{0,2,1:T(8,128)}, u32[]{:S(2)}) copy-start(f32[1024,1,64]{0,2,1:T(8,128)} %get-tuple-element.551) | copy-start | bytes 786436 | tf_op jit(solution)/shard_map/while
  972.1 7.6 copy-start.8
  972.1 8.3 copy-start.4
  995.2 340.7 %reduce-scatter.11.cloned.1.call-start = ((), (), s32[]{:S(2)}) async-start(), calls=%async_computation.13 | async-start | bytes 1179648 | tf_op jit(solution)/shard_map/reduce_scatter | solution.py:269
  1000.5 379.0 %reduce-scatter.9.cloned.1.call-start = ((), (), s32[]{:S(2)}) async-start(), calls=%async_computation.12 | async-start | bytes 4718592 | tf_op jit(solution)/shard_map/reduce_scatter | solution.py:268
  1007.4 427.0 %reduce-scatter.13.cloned.1.call-start = ((), (), s32[]{:S(2)}) async-start(), calls=%async_computation.14 | async-start | bytes 4718592 | tf_op jit(solution)/shard_map/reduce_scatter | solution.py:270
  1016.5 457.7 %reduce-scatter.19.cloned.1.call-start = ((), (), s32[]{:S(2)}) async-start(), calls=%async_computation.17 | async-start | bytes 1179648
  1292.3 272.0 %reduce-scatter.17.cloned.1.call-start = ((), (), s32[]{:S(2)}) async-start(), calls=%async_computation.16 | async-start | bytes 12976128 | tf_op jit(solution)/shard_map/reduce_scatter | solution.py:272
  1303.8 410.1 %reduce-scatter.15.cloned.1.call-start = ((), (), s32[]{:S(2)}) async-start(), calls=%async_computation.15 | async-start | bytes 25952256 | tf_op jit(solution)/shard_map/reduce_scatter | solution.py:271
  1718.4 48.7 %copy-start.10 = (f32[2,256,1408]{1,2,0:T(8,128)S(1)}, f32[2,256,1408]{1,2,0:T(8,128)}, u32[]{:S(2)}) copy-start(f32[2,256,1408]{1,2,0:T(8,128)} %reduce-scatter.15.cloned.1.call-done) | copy-start | bytes 8650756
  1783.2 7.1 copy-start.38
  1783.2 7.0 copy-start.39
  (55 other events, 178.7 us)
Sparse Core Ops, SparseCore 0:
  10.5 32.9 all-gather.4
  45.9 28.5 all-gather.6
  96.7 291.3 all-reduce.4
  390.5 66.6 all-gather.8
  459.5 44.3 all-gather.10
  539.2 290.8 all-reduce.6
  995.4 290.5 all-reduce.8
  1289.7 35.0 reduce-scatter.10
  1328.1 51.2 reduce-scatter.8
  1383.0 51.3 reduce-scatter.12
  1438.2 35.9 reduce-scatter.18
  1477.5 86.7 reduce-scatter.16
  1568.0 145.8 reduce-scatter.14
where the time goes:
time: 1810 us; the launch traced here: 1800 us
  waiting for transfers between devices  1280 us (71%)
  matrix products  218 us (12%)
  other arithmetic  120 us (7%)
  local copies, waits for them, and re-layouts  87.9 us (5%)
  blocking collectives  64.2 us (4%)
  between operations  22.3 us (1%)
    psum x1, waiting for transfers between devices, on_device(): branch = lax.psum(branch_partial, 'tensor')  287 us
    psum x1, waiting for transfers between devices, on_device(): grad_normed_two = lax.psum(partial_two, 'tensor')  280 us
    psum x1, waiting for transfers between devices, on_device(): lax.psum(jnp.dot(hidden, down_weight, preferred_element_type=jnp.float32)...  269 us
    reduce_scatter x1, waiting for transfers between devices, on_device(): lax.psum_scatter(grad_gateup_weight, 'dp', scatter_dimension=1, tiled=True)  147 us
    reduce_scatter x1, waiting for transfers between devices, on_device(): lax.psum_scatter(grad_down_weight, 'dp', scatter_dimension=1, tiled=True)  87.9 us
    all_gather x1, waiting for transfers between devices, on_device(): lax.all_gather(w_gateup.astype(jnp.bfloat16), 'dp', axis=1, tiled=True)  59.8 us
    reduce_scatter x1, waiting for transfers between devices, on_device(): lax.psum_scatter(grad_out_weight, 'dp', scatter_dimension=1, tiled=True)  51.9 us
    reduce_scatter x1, waiting for transfers between devices, on_device(): lax.psum_scatter(grad_query_weight, 'dp', scatter_dimension=0, tiled=True)  42 us
  transfers between devices with their start and end apart: 13, of which 10 were waited for; matrix products, arithmetic and copies ran while one was open for 10% of the time, Pallas kernels for 0%

commit v1 on v0

--- a/solution.py
+++ b/solution.py
@@ -14,6 +14,15 @@
 gain_rate = 0.2
 clip_limit = 1.0
 masked_value = -1000000000.0
+
+
+def doubling_sum(x, name):
+    size = lax.axis_size(name)
+    total, stride = (x, 1)
+    while stride < size:
+        total = total + lax.ppermute(total, name, [(i, i ^ stride) for i in range(size)])
+        stride = 2 * stride
+    return total
 
 
 def positions(segment):
@@ -165,7 +174,7 @@
     mixed_blocks, logsum_blocks = lax.map(forward_block, starts)
     mixture = mixed_blocks.reshape(length, local_heads * HD)
     branch_partial = jnp.dot(mixture, out_weight, preferred_element_type=jnp.float32)
-    branch = lax.psum(branch_partial, "tensor")
+    branch = doubling_sum(branch_partial, "tensor")
     middle = values_in + branch
     inverse_two = lax.rsqrt(jnp.mean(middle * middle, axis=-1, keepdims=True) + norm_eps)
     unit_two = middle * inverse_two

time: 1810 us -> 1990 us (1.099)
  waiting for transfers between devices: 1280 us -> 1450 us
    ppermute x0 -> x2, waiting for transfers between devices: none -> 541 us  [doubling_sum(): lax.ppermute(total, name, [(i, i ^ stride) for i in range(size)])]
    psum x1 -> x0, waiting for transfers between devices: 287 us -> none  [on_device(): branch = lax.psum(branch_partial, 'tensor')]
    all_gather x1, waiting for transfers between devices: 59.8 us -> 0.02 us  [on_device(): lax.all_gather(w_gateup.astype(jnp.bfloat16), 'dp', axis=1, tiled=True)]
    all_gather x1, waiting for transfers between devices: 26.5 us -> 0.01 us  [on_device(): lax.all_gather(w_down.astype(jnp.bfloat16), 'dp', axis=1, tiled=True)]
  transfers between devices with their start and end apart: 13 -> 14, of which waited for: 10 -> 9; matrix products, arithmetic and copies ran while one was open for 10% -> 10% of each run, Pallas kernels for 0% -> 0%
where the time goes in v1:
time: 1990 us; the launch traced here: 1980 us
  waiting for transfers between devices  1450 us (73%)
  matrix products  218 us (11%)
  other arithmetic  131 us (7%)
  local copies, waits for them, and re-layouts  86.4 us (4%)
  blocking collectives  64.8 us (3%)
  between operations  22.6 us (1%)
    ppermute x2, waiting for transfers between devices, doubling_sum(): lax.ppermute(total, name, [(i, i ^ stride) for i in range(size)])  541 us
    psum x1, waiting for transfers between devices, on_device(): grad_normed_two = lax.psum(partial_two, 'tensor')  280 us
    psum x1, waiting for transfers between devices, on_device(): lax.psum(jnp.dot(hidden, down_weight, preferred_element_type=jnp.float32)...  269 us
    reduce_scatter x1, waiting for transfers between devices, on_device(): lax.psum_scatter(grad_gateup_weight, 'dp', scatter_dimension=1, tiled=True)  147 us
    reduce_scatter x1, waiting for transfers between devices, on_device(): lax.psum_scatter(grad_down_weight, 'dp', scatter_dimension=1, tiled=True)  88.1 us
    reduce_scatter x1, waiting for transfers between devices, on_device(): lax.psum_scatter(grad_out_weight, 'dp', scatter_dimension=1, tiled=True)  52 us
    reduce_scatter x1, waiting for transfers between devices, on_device(): lax.psum_scatter(grad_query_weight, 'dp', scatter_dimension=0, tiled=True)  42.1 us
    dynamic_update_slice x4, local copies, waits for them, and re-layouts, on_device(): lax.scan(backward_block, (zero_rows, zero_rows), (starts, logsum_blocks))  41.2 us
  transfers between devices with their start and end apart: 14, of which 9 were waited for; matrix products, arithmetic and copies ran while one was open for 10% of the time, Pallas kernels for 0%

profile of v1, /device:TPU:0, one launch (start us, length us, event | category | flops | bytes accessed | tf_op | source)
XLA Modules:
  0.0 1983.5 jit_solution(13096602555428225069)
XLA Ops:
  14.1 10.6 all_gather.24
  28.5 14.7 all_gather.26
  54.8 37.3 %while.28 = (s32[]{:T(128)}, bf16[2,512,512]{2,1,0:T(8,128)(2,1)S(1)}, f32[2,1,8,512]{3,2,1,0:T(8,128)}, s32[2]{0:T(128)S(1)}, s32[1024]{0:T(1024)S(1)}, /*index...) while((s32[]{:T(128)}, ...), condition=%wide.region_6.7_spmd.clone, body=%wide.region_3.6_spmd.clone.sunk | while | flops 1125904896 | bytes 55982772 | solution.py:174
  101.3 181.3 %collective-permute-done = f32[1024,2048]{1,0:T(8,128)} collective-permute-done((f32[1024,2048]{1,0:T(8,128)S(1)}, f32[1024,2048]{1,0:T(8,128)}, u32[]{:S(2)}, u32[]{:S(2)}) %collective-permute-start) | collective-permute-done | bytes 8388640 | tf_op jit(solution)/shard_map/ppermute | solution.py:23
  282.6 11.9 add.263
  297.9 359.4 %collective-permute-done.1 = f32[1024,2048]{1,0:T(8,128)} collective-permute-done((f32[1024,2048]{1,0:T(8,128)}, f32[1024,2048]{1,0:T(8,128)}, u32[]{:S(2)}, u32[]{:S(2)}) %collective-permute-start.1) | collective-permute-done | bytes 8388640 | tf_op jit(solution)/shard_map/ppermute | solution.py:23
  657.4 12.0 multiply_reduce_fusion.2
  669.5 20.0 %convolution_bitcast_fusion.3 = f32[2,1024,1408]{2,1,0:T(8,128)} fusion(bf16[2,2048,1408]{2,1,0:T(8,128)(2,1)} %all-gather.9.cloned.1.call-done, f32[1024,2048]{1,0:T(8,128)} %get-tuple-element.339, f32[2048]{0:T(1024)S(1)} %bitcast.364, f32[1024]{0:T(1024)S(1)} %add_rsqrt_fusion), kind=kOutput, calls=%fused_computation.85 | convolution fusion | flops 11817451520 | bytes 31469568 | tf_op jit(solution)/shard_map/nd,sdf->snf/dot_general | solution.py:182
  689.5 15.6 fusion.71
  707.7 17.1 convolution_bitcast_fusion.4
  724.9 10.9 convolution_convert_fusion
  735.8 280.0 %all-reduce.4.cloned.1.call-done = f32[1024,2048]{1,0:T(8,128)} async-done(((f32[1024,2048]{1,0:T(8,128)}), f32[1024,2048]{1,0:T(8,128)}) %all-reduce.4.cloned.1.call-update) | async-done | bytes 8388624 | tf_op jit(solution)/shard_map/psum | solution.py:215
  1015.8 7.6 multiply_reduce_fusion
  1033.7 130.4 %while.29 = (s32[]{:T(128)}, f32[1024,1,64]{0,2,1:T(8,128)S(1)}, f32[1024,1,64]{0,2,1:T(8,128)S(1)}, f32[2,512,1,8,64]{1,0,4,3,2:T(2,128)}, s32[2]{0:T(128)S(1)}...) while((s32[]{:T(128)}, f32[1024,1,64]{0,2,1:T(8,128)S(1)}, ...), condition=%wide.region_13.14_spmd.clone, body=%wide.region_11.13_spmd.clone.sunk | while | flops 2728129024 | bytes 182942096 | solution.py:251
  1043.0 11.5 fusion.181
  1066.6 19.5 dynamic_update_slice.22
  1091.5 7.5 fusion.184
  1107.9 11.5 fusion.181
  1131.6 19.5 dynamic_update_slice.22
  1156.4 7.5 fusion.184
  1191.2 7.8 fusion.78
  1199.1 269.4 %all-reduce.6.cloned.1.call-done = (bf16[1024,2048]{1,0:T(8,128)(2,1)}, bf16[1024,2048]{1,0:T(8,128)(2,1)}) async-done(((bf16[1024,2048]{1,0:T(8,128)(2,1)}, bf16[1024,2048]{1,0:T(8,128)(2,1)}), (bf16[1024,2048]{1,0:T(8,128)(2,1)}, bf16[1024,2048]{1,0:T(8,128)(2,1)})) %all-reduce.6.cloned.1.call-update) | async-done | bytes 8388624 | tf_op jit(solution)/shard_map/psum | solution.py:186
  1475.0 11.4 fusion.124
  1487.1 20.8 %convolution_bitcast_fusion.2 = f32[2,2048,1408]{1,2,0:T(8,128)} fusion(bf16[1,1024,1408]{2,1,0:T(8,128)(2,1)} %copy-done.58, bf16[1,1024,1408]{2,1,0:T(8,128)(2,1)} %copy-done.57, f32[1024,2048]{1,0:T(8,128)} %get-tuple-element.339, f32[2048]{0:T(1024)S(1)} %bitcast.367, f32[1024]{0:T(1024)S(1)} %copy-done.47), kind=kOutput, calls=%fused_computation.61 | convolution fusion | flops 11820335104 | bytes 37236736 | tf_op jit(solution)/shard_map/nd,snf->sdf/dot_general | solution.py:209
  1520.0 42.1 %reduce-scatter.9.cloned.1.call-done = f32[256,512]{1,0:T(8,128)} async-done(((f32[2048,512]{1,0:T(8,128)}), f32[256,512]{1,0:T(8,128)}) %reduce-scatter.9.cloned.1.call-update) | async-done | bytes 524304 | tf_op jit(solution)/shard_map/reduce_scatter | solution.py:277
  1565.1 52.0 %reduce-scatter.13.cloned.1.call-done = f32[512,256]{1,0:T(8,128)} async-done(((f32[512,2048]{1,0:T(8,128)}), f32[512,256]{1,0:T(8,128)}) %reduce-scatter.13.cloned.1.call-update) | async-done | bytes 524304 | tf_op jit(solution)/shard_map/reduce_scatter | solution.py:279
  1619.6 9.5 fusion.60
  1629.1 27.7 %reduce-scatter.19.cloned.1.call-done = f32[256,2]{1,0:T(8,128)} async-done(((f32[2048,2]{1,0:T(8,128)}), f32[256,2]{1,0:T(8,128)}) %reduce-scatter.19.cloned.1.call-update) | async-done | bytes 2064
  1659.0 88.1 %reduce-scatter.17.cloned.1.call-done = f32[1408,256]{1,0:T(8,128)} async-done(((f32[1408,2048]{1,0:T(8,128)}), f32[1408,256]{1,0:T(8,128)}) %reduce-scatter.17.cloned.1.call-update) | async-done | bytes 1441808 | tf_op jit(solution)/shard_map/reduce_scatter | solution.py:281
  1749.4 147.1 %reduce-scatter.15.cloned.1.call-done = f32[2,256,1408]{1,2,0:T(8,128)} async-done(((f32[2,2048,1408]{1,2,0:T(8,128)}), f32[2,256,1408]{1,2,0:T(8,128)}) %reduce-scatter.15.cloned.1.call-update) | async-done | bytes 2883600 | tf_op jit(solution)/shard_map/reduce_scatter | solution.py:280
  1901.0 8.4 add_convert_fusion
  1909.4 39.5 %psum.31 = f32[]{:T(128)} all-reduce(f32[]{:T(128)S(6)} %add.279), channel_id=1, replica_groups=mesh['dp'=8,'tensor'=4] {'dp','tensor'}, use_global_device_ids=true, to_apply=%region_30.31 | all-reduce | flops 1 | bytes 8 | tf_op jit(solution)/shard_map/psum | solution.py:287
  (276 shorter events, 209.7 us)
Async XLA Ops:
  7.2 41.4 %all-gather.5.cloned.1.call-start = ((), (), s32[]{:S(2)}) async-start(), calls=%async_computation.6 | async-start | bytes 2359296 | tf_op jit(solution)/shard_map/all_gather | solution.py:113
  9.1 83.0 %all-gather.7.cloned.1.call-start = ((), (), s32[]{:S(2)}) async-start(), calls=%async_computation.7 | async-start | bytes 2359296 | tf_op jit(solution)/shard_map/all_gather | solution.py:115
  10.9 17.6 copy-start.33
  10.9 658.5 %all-gather.9.cloned.1.call-start = ((), (), s32[]{:S(2)}) async-start(), calls=%async_computation.8 | async-start | bytes 12976128 | tf_op jit(solution)/shard_map/all_gather | solution.py:116
  14.0 675.5 %all-gather.11.cloned.1.call-start = ((), (), s32[]{:S(2)}) async-start(), calls=%async_computation.9 | async-start | bytes 6488064 | tf_op jit(solution)/shard_map/all_gather | solution.py:117
  14.1 29.1 %copy-start.4 = (bf16[1024,2048]{1,0:T(8,128)(2,1)S(1)}, bf16[1024,2048]{1,0:T(8,128)(2,1)}, u32[]{:S(2)}) copy-start(bf16[1024,2048]{1,0:T(8,128)(2,1)} %param.26) | copy-start | bytes 12582916
  25.4 23.3 %copy-start.42 = (f32[1,2048]{1,0:T(1,128)}, f32[1,2048]{1,0:T(1,128)S(1)}, u32[]{:S(2)}) copy-start(f32[1,2048]{1,0:T(1,128)S(1)} %get-tuple-element.356) | copy-start | bytes 24580
  28.5 20.2 %copy-start.48 = (f32[1024]{0:T(1024)}, f32[1024]{0:T(1024)S(1)}, u32[]{:S(2)}) copy-start(f32[1024]{0:T(1024)S(1)} %add_rsqrt_fusion.1) | copy-start | bytes 12292
  99.8 197.1 %copy-start.14 = (f32[1408,256]{1,0:T(8,128)S(1)}, f32[1408,256]{1,0:T(8,128)}, u32[]{:S(2)}) copy-start(f32[1408,256]{1,0:T(8,128)} %param.45) | copy-start | bytes 4325380
  99.8 182.8 %collective-permute-start = (f32[1024,2048]{1,0:T(8,128)S(1)}, f32[1024,2048]{1,0:T(8,128)}, u32[]{:S(2)}, u32[]{:S(2)}) collective-permute-start(f32[1024,2048]{1,0:T(8,128)S(1)} %fusion.122), channel_id=1, source_target_pairs={{0,1},{1,0},{2,3},{3,2},{4,5},{5,4},{6,7},{7,6},{8,9},{9,8},{10,11... | collective-permute-start | bytes 25165832 | tf_op jit(solution)/shard_map/ppermute | solution.py:23
  294.5 362.9 %collective-permute-start.1 = (f32[1024,2048]{1,0:T(8,128)}, f32[1024,2048]{1,0:T(8,128)}, u32[]{:S(2)}, u32[]{:S(2)}) collective-permute-start(f32[1024,2048]{1,0:T(8,128)} %add.263), channel_id=1, source_target_pairs={{0,2},{1,3},{2,0},{3,1},{4,6},{5,7},{6,4},{7,5},{8,10},{9,11},{10,... | collective-permute-start | bytes 25165832 | tf_op jit(solution)/shard_map/ppermute | solution.py:23
  297.9 371.6 %copy-start.44 = (f32[1,2048]{1,0:T(1,128)S(1)}, f32[1,2048]{1,0:T(1,128)}, u32[]{:S(2)}) copy-start(f32[1,2048]{1,0:T(1,128)} %get-tuple-element.355) | copy-start | bytes 24580
  297.9 717.9 %all-reduce.4.cloned.1.call-start = ((), (), s32[]{:S(2)}) async-start(), calls=%async_computation.10 | async-start | bytes 16777216 | tf_op jit(solution)/shard_map/psum | solution.py:215
  669.4 354.0 %copy-start.46 = (f32[1024]{0:T(1024)}, f32[1024]{0:T(1024)S(1)}, u32[]{:S(2)}) copy-start(f32[1024]{0:T(1024)S(1)} %add_rsqrt_fusion) | copy-start | bytes 12292
  724.8 743.7 %all-reduce.6.cloned.1.call-start = ((), (), s32[]{:S(2)}) async-start(), calls=%async_computation.17 | async-start | bytes 16777216 | tf_op jit(solution)/shard_map/psum | solution.py:186
  1015.8 8.2 copy-start.7
  1015.8 9.4 copy-start.15
  1091.5 7.6 copy-start.2
  1091.5 7.6 copy-start.6
  1156.4 7.6 copy-start.2
  1156.4 7.6 copy-start.6
  1177.8 340.6 %reduce-scatter.11.cloned.1.call-start = ((), (), s32[]{:S(2)}) async-start(), calls=%async_computation.12 | async-start | bytes 1179648 | tf_op jit(solution)/shard_map/reduce_scatter | solution.py:278
  1183.1 379.0 %reduce-scatter.9.cloned.1.call-start = ((), (), s32[]{:S(2)}) async-start(), calls=%async_computation.11 | async-start | bytes 4718592 | tf_op jit(solution)/shard_map/reduce_scatter | solution.py:277
  1190.0 427.1 %reduce-scatter.13.cloned.1.call-start = ((), (), s32[]{:S(2)}) async-start(), calls=%async_computation.13 | async-start | bytes 4718592 | tf_op jit(solution)/shard_map/reduce_scatter | solution.py:279
  1199.1 457.7 %reduce-scatter.19.cloned.1.call-start = ((), (), s32[]{:S(2)}) async-start(), calls=%async_computation.16 | async-start | bytes 1179648
  1474.9 272.1 %reduce-scatter.17.cloned.1.call-start = ((), (), s32[]{:S(2)}) async-start(), calls=%async_computation.15 | async-start | bytes 12976128 | tf_op jit(solution)/shard_map/reduce_scatter | solution.py:281
  1486.4 410.1 %reduce-scatter.15.cloned.1.call-start = ((), (), s32[]{:S(2)}) async-start(), calls=%async_computation.14 | async-start | bytes 25952256 | tf_op jit(solution)/shard_map/reduce_scatter | solution.py:280
  1901.0 48.7 %copy-start.9 = (f32[2,256,1408]{1,2,0:T(8,128)S(1)}, f32[2,256,1408]{1,2,0:T(8,128)}, u32[]{:S(2)}) copy-start(f32[2,256,1408]{1,2,0:T(8,128)} %reduce-scatter.15.cloned.1.call-done) | copy-start | bytes 8650756
  1965.8 7.1 copy-start.34
  1965.8 7.0 copy-start.35
  1965.8 7.0 copy-start.40
  1965.8 7.0 copy-start.41
  (47 other events, 153.6 us)
Sparse Core Ops, SparseCore 0:
  10.5 33.1 all-gather.4
  46.2 28.3 all-gather.6
  77.0 67.6 all-gather.8
  298.0 42.5 all-gather.10
  725.0 290.8 all-reduce.3
  1177.9 290.5 all-reduce.5
  1472.3 35.0 reduce-scatter.10
  1510.7 51.2 reduce-scatter.8
  1565.8 51.3 reduce-scatter.12
  1620.7 35.9 reduce-scatter.18
  1660.3 86.7 reduce-scatter.16
  1750.5 145.9 reduce-scatter.14
